TPU v7x, 32 devices: a whole 2x2x4 slice. The times are simulated.
32 devices in a mesh: grp: 2 (over y), visit: 16 (over z, x, core).
Axes of the slice: x: 2, y: 2, z: 4, core: 2. Of those that a mesh axis runs over, the one named last changes fastest.
Arguments:
- science: float32 [8192, 1024], P(('grp', 'visit')), parts along dimension 0, may hold values from -6 to 6
- patches: float32 [256, 256, 256], P(('grp', 'visit')), parts along dimension 0, may hold values from -6 to 6
- margin: int32 [128, 3], P('grp'), parts along dimension 0, may hold values from 0 to 255, as said below
- kernel_coef: float32 [27, 128], P(None, ('grp', 'visit')), parts along dimension 1, may hold values from -4 to 4
- ccd_first: int32 [32], P('grp'), parts along dimension 0, may hold values 0 or 1
Outputs:
- patch_mean: float32 [256, 256, 256], P(('grp', 'visit')), parts along dimension 0
There are 2 independent parts, one for each index of `grp`. A program takes and returns all parts, laid end to end along the dimension named above; each array names one. Nothing has to cross between parts.
Inputs may be any that keep to these rules, and one draw needn't show every extreme that they name: `margin`: column 0 is a patch id, columns 1 and 2 are offsets below 256. A tile of strip d names a patch owned by strip d - 1, d or d + 1. Among the 4 tiles of one strip at most 2 name patches of one owner (patch id // 8), and in every strip some owner is named exactly 2 times.
All inputs are finite; a program needn't handle non-finite values.
Results may differ from a plain program's by a relative error of at most 0.004.
Values may be sent and summed in bfloat16 or wider, within the bound.
No kernel may reach another device: no remote copies, remote signals or barrier semaphores. Data moves between devices by JAX's collectives and lax.ppermute only.
A program may use at most 64 MiB of HBM per device.

v0:
```python
import functools

import jax
import jax.numpy as jnp
import numpy as np
from jax import lax
from jax.experimental import pallas as pl
from jax.experimental.pallas import tpu as pltpu
from jax.sharding import PartitionSpec as P

TILE = 256
HALF = 128
RADIUS = 10
SIGMAS = 3
ORDERS = 3
EDGE = 16
CAP = 2
STRIPS = 3
SLOTS = STRIPS * CAP
KINDS = 4
TOP, BOTTOM, LEFT, RIGHT = range(KINDS)
PIECES = SLOTS * KINDS
COEF_ROWS = 16
NEAR = 8
PIECE_ROWS = CAP * EDGE
NEAR_ROWS = COEF_ROWS + NEAR * CAP * RADIUS
TWO_ROWS = (STRIPS * KINDS - NEAR) * CAP * RADIUS
RECORD = COEF_ROWS + PIECES * EDGE
MEMBERS = 7
ENTRY = 16
HEAD = 2
REACH = HALF + 2 * EDGE


def owned_slots(margin, owner, strips, per_strip, owned):
    slots = []
    for q in range(STRIPS):
        strip = owner - 1 + q
        inside = (strip >= 0) & (strip < strips)
        base = jnp.clip(strip, 0, strips - 1) * per_strip
        count = jnp.int32(0)
        found = [jnp.int32(-1) for _ in range(CAP)]
        for s in range(per_strip):
            mine = inside & (owner_of(margin[0, base + s], owned) == owner)
            for j in range(CAP):
                found[j] = jnp.where(mine & (count == j), base + s, found[j])
            count = count + jnp.where(mine, 1, 0)
        slots.extend(found)
    return slots


def sign_of(owner):
    return 1 - 2 * lax.rem(owner, 2)


def piece_position(relative, kind, sign):
    along = relative * sign
    facing = jnp.where(sign > 0, kind, jnp.where(kind == TOP, BOTTOM, jnp.where(kind == BOTTOM, TOP, kind)))
    middle = jnp.where(facing == TOP, 4, jnp.where(facing == BOTTOM, 11, facing + 3))
    return jnp.where(along < 0, facing, jnp.where(along > 0, 7 + facing, middle))


def owner_of(patch, owned):
    if owned & (owned - 1) == 0:
        return lax.shift_right_logical(patch, jnp.int32(owned.bit_length() - 1))
    return lax.div(patch, owned)


def packed(record, first, count):
    rows = record[COEF_ROWS + first * EDGE : COEF_ROWS + (first + count) * EDGE, :].astype(jnp.float32)
    return jnp.concatenate([rows[n * EDGE : n * EDGE + RADIUS] for n in range(count)], axis=0).astype(jnp.bfloat16)


def spaced(rows):
    rows = rows.astype(jnp.float32)
    empty = jnp.zeros((EDGE - RADIUS, TILE), jnp.float32)
    pieces = []
    for n in range(rows.shape[0] // RADIUS):
        pieces += [rows[n * RADIUS : (n + 1) * RADIUS], empty]
    return jnp.concatenate(pieces, axis=0).astype(jnp.bfloat16)


def pack_kernel(sizes, margin_hbm, coef_hbm, patches, science, aligned, to_chip, to_next, to_two, to_far,
                margin, coef, patch_buf, science_buf, slot_of, patch_sem, science_sem, small_sem):
    strips, per_strip, owned = sizes
    tables = [
        pltpu.make_async_copy(a, b, small_sem.at[n]) for n, (a, b) in enumerate(((margin_hbm, margin), (coef_hbm, coef)))
    ]
    for copy in tables:
        copy.start()
    whole = pltpu.make_async_copy(science, science_buf, science_sem)
    whole.start()
    to_chip[COEF_ROWS:RECORD, :] = jnp.zeros((RECORD - COEF_ROWS, TILE), jnp.bfloat16)
    to_far[...] = jnp.zeros(to_far.shape, jnp.bfloat16)
    for copy in tables:
        copy.wait()
    owner = lax.axis_index("visit")
    sign = sign_of(owner)
    slots = owned_slots(margin, owner, strips, per_strip, owned)
    for k in range(SLOTS):
        slot_of[k] = slots[k]

        @pl.when(slots[k] >= 0)
        def _(k=k):
            local = lax.rem(margin[0, jnp.maximum(slots[k], 0)], owned)
            pltpu.make_async_copy(patches.at[local], patch_buf.at[k], patch_sem.at[k]).start()

    values = coef[...]
    bases = values.shape[1]
    high = values.astype(jnp.bfloat16).astype(jnp.float32)
    middle = (values - high).astype(jnp.bfloat16).astype(jnp.float32)
    low = values - high - middle
    parts = jnp.concatenate([high, middle, low, jnp.zeros_like(low)], axis=0).astype(jnp.bfloat16)
    to_chip[:COEF_ROWS, :bases] = parts
    to_next[:COEF_ROWS, :bases] = parts

    whole.wait()
    counts = [jnp.int32(0), jnp.int32(0)]
    for s in range(per_strip):
        tile = owner * per_strip + s
        offset = lax.div(margin[0, tile], owned) - owner

        @pl.when(offset != 0)
        def _(s=s, tile=tile, offset=offset, counts=tuple(counts)):
            up = lax.rem(TILE - margin[1, tile], TILE)
            back = lax.rem(TILE - margin[2, tile], TILE)
            moved = pltpu.roll(pltpu.roll(science_buf[:, s * TILE : (s + 1) * TILE], up, 0), back, 1)
            moved16 = moved.astype(jnp.bfloat16)

            @pl.when(offset == sign)
            def _():
                to_chip[pl.ds(pl.multiple_of(RECORD + counts[0] * TILE, EDGE), TILE), :] = moved16

            @pl.when(offset != sign)
            def _():
                to_next[pl.ds(pl.multiple_of(NEAR_ROWS + counts[1] * TILE, EDGE), TILE), :] = moved16

        counts[0] = counts[0] + jnp.where(offset == sign, 1, 0)
        counts[1] = counts[1] + jnp.where(offset == -sign, 1, 0)

    def slot_step(k, carry):
        tile = slot_of[k]

        @pl.when(tile >= 0)
        def _():
            down = margin[1, tile]
            right = margin[2, tile]
            local = lax.rem(margin[0, tile], owned)
            pltpu.make_async_copy(patches.at[local], patch_buf.at[k], patch_sem.at[k]).wait()
            moved = pltpu.roll(pltpu.roll(patch_buf[k], down, 0), right, 1)
            moved16 = moved.astype(jnp.bfloat16)
            aligned[k] = moved16
            relative = lax.div(k, CAP) - 1
            j = lax.rem(k, CAP)
            left = jnp.transpose(moved[:, :HALF])[:EDGE]
            right_edge = jnp.transpose(moved[:, TILE - HALF :])[HALF - RADIUS :]
            empty = jnp.zeros((EDGE - RADIUS, TILE), jnp.float32)
            bottom = jnp.concatenate([moved[TILE - RADIUS :], empty], axis=0)
            right_edge = jnp.concatenate([right_edge, empty], axis=0)
            edges = [moved16[:EDGE]] + [edge.astype(jnp.bfloat16) for edge in (bottom, left, right_edge)]
            for kind in range(KINDS):
                position = piece_position(relative, jnp.int32(kind), sign)
                row = pl.multiple_of(COEF_ROWS + (position * CAP + j) * EDGE, EDGE)
                to_chip[pl.ds(row, EDGE), :] = edges[kind]

                @pl.when(position == 0)
                def _(kind=kind):
                    to_far[pl.ds(pl.multiple_of(j * EDGE, EDGE), EDGE), :] = edges[kind]

        return carry

    lax.fori_loop(0, SLOTS, slot_step, 0)
    to_next[COEF_ROWS:NEAR_ROWS, :] = packed(to_chip, 0, NEAR * CAP)
    to_two[...] = packed(to_chip, NEAR * CAP, PIECES - NEAR * CAP)


def profile(u, sigma, order):
    taps = np.arange(-RADIUS, RADIUS + 1).astype(np.float32)
    total = float(np.sum(np.exp(-taps * taps / np.float32(2.0 * sigma * sigma)), dtype=np.float32))
    shape = jnp.where(jnp.abs(u) <= RADIUS, jnp.exp(-u * u / (2.0 * sigma * sigma)) / total, 0.0)
    for _ in range(order):
        shape = shape * (u / sigma)
    return shape


def fill_tables(across, mixing):
    w = lax.broadcasted_iota(jnp.int32, (TILE, HALF), 0) - lax.broadcasted_iota(jnp.int32, (TILE, HALF), 1)
    w = jnp.where(w > HALF, w - TILE, w).astype(jnp.float32)
    for g in range(SIGMAS):
        for h in range(ORDERS):
            n = g * ORDERS + h
            across[:, n * HALF : (n + 1) * HALF] = profile(w, 0.75 * 2.0**g, h).astype(jnp.bfloat16)
    lanes = SIGMAS * ORDERS * REACH
    for at in range(0, lanes, HALF):
        wide = min(HALF, lanes - at)
        lane = lax.broadcasted_iota(jnp.int32, (HALF, wide), 1) + at
        row = lax.broadcasted_iota(jnp.int32, (HALF, wide), 0)
        one = at // REACH
        two = (at + wide - 1) // REACH
        start = jnp.where(lane < two * REACH, one * REACH, two * REACH)
        u = (lane - start - row - EDGE).astype(jnp.float32)
        low, high = one // ORDERS, two // ORDERS
        sigma = 0.75 * 2.0**low
        if high != low:
            sigma = jnp.where(lane < two * REACH, sigma, 0.75 * 2.0**high)
        totals = []
        for g in (low, high):
            taps = np.arange(-RADIUS, RADIUS + 1).astype(np.float32)
            totals.append(float(np.sum(np.exp(-taps * taps / np.float32(2.0 * (0.75 * 2.0**g) ** 2)), dtype=np.float32)))
        total = totals[0] if high == low else jnp.where(lane < two * REACH, totals[0], totals[1])
        shape = jnp.where(jnp.abs(u) <= RADIUS, jnp.exp(-u * u / (2.0 * sigma * sigma)) / total, 0.0)
        for v in range(ORDERS):
            mixing[v, :, at : at + wide] = shape
            shape = shape * (u / sigma)


def plan_kernel(sizes, margin, ccd_first, from_chip, science, plan, across, mixing, first, rows):
    strips, per_strip, owned = sizes
    owner = lax.axis_index("visit")
    sign = sign_of(owner)
    slots = owned_slots(margin, owner, strips, per_strip, owned)
    ids = [jnp.where(t >= 0, margin[0, jnp.maximum(t, 0)], -1) for t in slots]
    counts = [sum(jnp.where(other == mine, 1, 0) for other in ids) for mine in ids]
    entry = jnp.int32(0)
    places = []
    for k in range(SLOTS):
        places.append(entry)
        entry = entry + jnp.where(slots[k] >= 0, 1, 0)
        plan[k] = slots[k]
        plan[SLOTS + k] = counts[k]
        plan[2 * SLOTS + k] = places[k]
    plan[3 * SLOTS] = entry

    for i in range(2 * STRIPS - 1):
        strip = jnp.clip(owner - STRIPS + 1 + i, 0, strips - 1)
        owners = [owner_of(margin[0, strip * per_strip + n], owned) for n in range(per_strip)]
        for n, its_owner in enumerate(owners):
            rank = sum((jnp.where(other == its_owner, 1, 0) for other in owners[:n]), jnp.int32(0))
            start = ((its_owner - owner) * sign + 3) * RECORD + COEF_ROWS + rank * EDGE
            its_sign = sign_of(its_owner)
            for kind in range(KINDS):
                place = piece_position(strip - its_owner, jnp.int32(kind), its_sign)
                rows[(i * per_strip + n) * KINDS + kind] = start + place * PIECE_ROWS

    def piece_row(strip, position, kind, allowed):
        inside = (position >= 0) & (position < per_strip) & allowed
        at = ((strip - owner + STRIPS - 1) * per_strip + position) * KINDS + kind
        return jnp.where(inside, rows[jnp.where(inside, at, 0)], MEMBERS * RECORD)

    def fill(k, carry):
        tile = plan[k]

        @pl.when(tile >= 0)
        def _():
            q = lax.div(k, CAP)
            j = lax.rem(k, CAP)
            strip = owner - 1 + q
            position = tile - strip * per_strip
            local = lax.rem(margin[0, tile], owned)
            up = lax.rem(TILE - margin[1, tile], TILE)
            back = lax.rem(TILE - margin[2, tile], TILE)
            yes = owner >= 0
            keep_top = (strip > 0) & (ccd_first[strip] == 0)
            keep_bottom = (strip < strips - 1) & (ccd_first[jnp.minimum(strip + 1, strips - 1)] == 0)
            at = ENTRY * (plan[2 * SLOTS + k] + HEAD)
            member = (q - 1) * sign
            pieces = (
                (strip, position + 1, LEFT, yes),
                (strip, position - 1, RIGHT, yes),
                (strip - 1, position, BOTTOM, keep_top),
                (strip - 1, position - 1, BOTTOM, keep_top),
                (strip - 1, position + 1, BOTTOM, keep_top),
                (strip + 1, position, TOP, keep_bottom),
                (strip + 1, position - 1, TOP, keep_bottom),
                (strip + 1, position + 1, TOP, keep_bottom),
            )
            for n, args in enumerate(pieces):
                plan[at + n] = piece_row(*args)
            plan[at + 8] = k
            plan[at + 9] = up
            plan[at + 10] = back
            plan[at + 11] = local
            plan[at + 12] = plan[SLOTS + k]
            plan[at + 13] = member + 3
            plan[at + 14] = position
            share = share_of(plan[SLOTS + k])

            @pl.when(member == 0)
            def _():
                start = pl.multiple_of(position * TILE, TILE)
                moved = pltpu.roll(pltpu.roll(science[:, pl.ds(start, TILE)], up, 0), back, 1)
                first[local] = first[local] + moved * share

            @pl.when(member == 1)
            def _():
                start = pl.multiple_of(RECORD + j * TILE, EDGE)
                first[local] = first[local] + from_chip[pl.ds(start, TILE), :].astype(jnp.float32) * share

        return carry

    first[...] = jnp.zeros(first.shape, jnp.float32)
    lax.fori_loop(0, SLOTS, fill, 0)
    fill_tables(across, mixing)


def share_of(count):
    share = jnp.float32(1.0)
    for n in range(2, SLOTS + 1):
        share = jnp.where(count == n, jnp.float32(1.0 / n), share)
    return share


def match_kernel(per_strip, plan, aligned, own_record, from_chip, from_next, from_two, from_across, from_far,
                 across, mixing, first, out,
                 frames, window, spread, mixes, total):
    def put(member, start, rows, value):
        frames[member * RECORD + start : member * RECORD + start + rows, :] = value

    near = NEAR * PIECE_ROWS
    put(0, COEF_ROWS, PIECE_ROWS, from_far[...])
    put(1, COEF_ROWS + near, RECORD - COEF_ROWS - near, spaced(from_two[...]))
    put(2, 0, COEF_ROWS, from_next[:COEF_ROWS, :])
    put(2, COEF_ROWS, near, spaced(from_next[COEF_ROWS:NEAR_ROWS, :]))
    put(3, 0, RECORD, own_record[:RECORD, :])
    put(4, 0, RECORD, from_chip[:RECORD, :])
    put(5, COEF_ROWS, near, spaced(from_across[COEF_ROWS:NEAR_ROWS, :]))
    put(6, COEF_ROWS + near, RECORD - COEF_ROWS - near, spaced(from_across[NEAR_ROWS:, :]))
    put(MEMBERS, 0, EDGE, jnp.zeros((EDGE, TILE), jnp.bfloat16))
    columns = SIGMAS * ORDERS
    window_rows = TILE + 2 * EDGE
    out[...] = first[...]
    total[...] = jnp.zeros(total.shape, jnp.float32)
    strip_lanes = per_strip

    def base(k):
        return ENTRY * (k + HEAD)

    def lowered(edge):
        empty = jnp.zeros((EDGE - RADIUS, TILE), jnp.float32)
        return jnp.concatenate([empty, edge.astype(jnp.float32)[:RADIUS]], axis=0).astype(jnp.bfloat16)

    def build(k, half):
        at = base(k)

        def piece(n):
            return frames[pl.ds(pl.multiple_of(plan[at + n], EDGE), EDGE), :]

        sides = jnp.concatenate(
            [
                piece(0).astype(jnp.float32),
                jnp.zeros((HALF - EDGE - RADIUS, TILE), jnp.float32),
                piece(1).astype(jnp.float32)[:RADIUS],
            ],
            axis=0,
        )
        sides = jnp.transpose(sides).astype(jnp.bfloat16)

        def place(start, rows, middle_a, middle_b, left_b, right_a):
            low = lax.broadcasted_iota(jnp.int32, (rows, HALF), 1) < HALF // 2
            window[half, start : start + rows, :HALF] = middle_a
            window[half, start : start + rows, HALF:] = jnp.where(low, middle_b, left_b)
            second = window_rows + start
            window[half, second : second + rows, :HALF] = middle_b
            window[half, second : second + rows, HALF:] = jnp.where(low, right_a, middle_a)

        center = aligned[plan[at + 8]]
        place(EDGE, TILE, center[:, :HALF], center[:, HALF:], sides, sides)
        for start, n in ((0, 2), (EDGE + TILE, 5)):
            middle, left, right = piece(n), piece(n + 1), piece(n + 2)
            if start == 0:
                middle, left, right = lowered(middle), lowered(left), lowered(right)
            place(start, EDGE, middle[:, :HALF], middle[:, HALF:], left[:, HALF:], right[:, :HALF])

    def finish(k, half, share):
        at = base(k)
        local = plan[at + 11]
        back = pltpu.roll(pltpu.roll(total[half], plan[at + 9], 0), plan[at + 10], 1)
        out[local] = out[local] - back * share

    count = plan[3 * SLOTS]

    for k in range(SLOTS):
        @pl.when((plan[k] >= 0) & (plan[base(plan[2 * SLOTS + k]) + 13] == 2))
        def _(k=k):
            at = base(plan[2 * SLOTS + k])
            local = plan[at + 11]
            start = NEAR_ROWS + (k % CAP) * TILE
            arrived = from_next[start : start + TILE, :].astype(jnp.float32)
            out[local] = out[local] + arrived * share_of(plan[at + 12])

    @pl.when(count > 0)
    def _():
        build(0, 0)

    def step(k, carry):
        half = lax.rem(k, 2)
        at = base(k)
        coef_row = pl.multiple_of(plan[at + 13] * RECORD, EDGE)
        block = frames[pl.ds(coef_row, COEF_ROWS), :HALF].astype(jnp.float32)
        rows = lax.broadcasted_iota(jnp.int32, block.shape, 0)
        mine = (lax.rem(rows, strip_lanes) == plan[at + 14]) & (rows < 3 * strip_lanes)
        weights = jnp.sum(jnp.where(mine, block, 0.0), axis=0, keepdims=True)
        lanes = columns * REACH
        for n in range(0, columns, 2):
            if n == 2:
                finish(jnp.maximum(k - 1, 0), 1 - half, jnp.where(k > 0, share_of(plan[base(jnp.maximum(k - 1, 0)) + 12]), 0.0))
            if n == 4:
                build(jnp.minimum(k + 1, count - 1), 1 - half)
            wide = min(2, columns - n)
            h = jnp.dot(window[half], across[:, n * HALF : (n + wide) * HALF], preferred_element_type=jnp.float32)
            h = h.astype(jnp.bfloat16)
            for m in range(wide):
                to = (n + m) * REACH
                for c in range(2):
                    for r in range(2):
                        start = c * window_rows + r * HALF
                        spread[r, to : to + REACH, c * HALF : (c + 1) * HALF] = h[
                            start : start + REACH, m * HALF : (m + 1) * HALF
                        ]
            for at in range(n * REACH // HALF * HALF, min(lanes, (n + 2) * REACH // HALF * HALF), HALF):
                wide_at = min(HALF, lanes - at)
                lane = lax.broadcasted_iota(jnp.int32, (1, wide_at), 1) + at
                mix = jnp.zeros((HALF, wide_at), jnp.float32)
                one = at // REACH
                two = min((at + wide_at - 1) // REACH, columns - 1)
                for v in range(ORDERS):
                    weight = weights[:, one * ORDERS + v : one * ORDERS + v + 1]
                    if two != one:
                        other = weights[:, two * ORDERS + v : two * ORDERS + v + 1]
                        weight = jnp.where(lane < two * REACH, weight, other)
                    mix = mix + weight * mixing[v, :, at : at + wide_at]
                mixes[:, at : at + wide_at] = mix.astype(jnp.bfloat16)
        for r in range(2):
            total[half, r * HALF : (r + 1) * HALF, :] = jnp.dot(
                mixes[...], spread[r], preferred_element_type=jnp.float32
            )
        return carry

    lax.fori_loop(0, count, step, 0)

    @pl.when(count > 0)
    def _():
        finish(count - 1, lax.rem(count - 1, 2), share_of(plan[base(count - 1) + 12]))


def step(science, patches, margin, kernel_coef, ccd_first):
    strips = lax.axis_size("visit")
    owned = patches.shape[0]
    per_strip = science.shape[1] // TILE
    sizes = (strips, per_strip, owned)
    margin = margin.T
    smem = pl.BlockSpec(memory_space=pltpu.SMEM)
    vmem = pl.BlockSpec(memory_space=pltpu.VMEM)
    hbm = pl.BlockSpec(memory_space=pl.ANY)
    stays = pl.BlockSpec(memory_space=pltpu.HBM)
    bf16 = jnp.bfloat16
    f32 = jnp.float32
    aligned, to_chip, to_next, to_two, to_far = pl.pallas_call(
        functools.partial(pack_kernel, sizes),
        out_shape=(
            jax.ShapeDtypeStruct((SLOTS, TILE, TILE), bf16),
            jax.ShapeDtypeStruct((RECORD + CAP * TILE, TILE), bf16),
            jax.ShapeDtypeStruct((NEAR_ROWS + CAP * TILE, TILE), bf16),
            jax.ShapeDtypeStruct((TWO_ROWS, TILE), bf16),
            jax.ShapeDtypeStruct((PIECE_ROWS, TILE), bf16),
        ),
        in_specs=[stays] * 4,
        out_specs=(vmem, vmem, vmem, vmem, vmem),
        scratch_shapes=[
            pltpu.SMEM(margin.shape, jnp.int32),
            pltpu.VMEM(kernel_coef.shape[::-1], f32),
            pltpu.VMEM((SLOTS, TILE, TILE), f32),
            pltpu.VMEM((TILE, per_strip * TILE), f32),
            pltpu.SMEM((SLOTS,), jnp.int32),
            pltpu.SemaphoreType.DMA((SLOTS,)),
            pltpu.SemaphoreType.DMA,
            pltpu.SemaphoreType.DMA((2,)),
        ],
        compiler_params=pltpu.CompilerParams(vmem_limit_bytes=52 * 2**20),
        name="pack",
    )(margin, kernel_coef.T, patches, science)

    on_chip = [(i, i ^ 1) for i in range(strips)]
    next_chip = [p for i in range(1, strips - 1, 2) for p in ((i, i + 1), (i + 1, i))]
    far = [p for i in range(1, strips - 3, 2) for p in ((i, i + 3), (i + 3, i))]
    two = [p for i in range(0, strips - 2, 2) for p in ((i, i + 2), (i + 3, i + 1))]
    from_next = lax.ppermute(to_next, "visit", next_chip)
    from_two = lax.ppermute(to_two, "visit", two)
    from_far = lax.ppermute(to_far, "visit", far)
    from_chip = lax.ppermute(to_chip, "visit", on_chip)

    columns = SIGMAS * ORDERS
    planned = pl.pallas_call(
        functools.partial(plan_kernel, sizes),
        out_shape=(
            jax.ShapeDtypeStruct((ENTRY * (HEAD + SLOTS),), jnp.int32),
            jax.ShapeDtypeStruct((TILE, columns * HALF), bf16),
            jax.ShapeDtypeStruct((ORDERS, HALF, columns * REACH), f32),
            jax.ShapeDtypeStruct(patches.shape, f32),
        ),
        in_specs=[smem, smem] + [vmem] * 2,
        out_specs=(smem, vmem, vmem, vmem),
        scratch_shapes=[pltpu.SMEM(((2 * STRIPS - 1) * per_strip * KINDS,), jnp.int32)],
        compiler_params=pltpu.CompilerParams(vmem_limit_bytes=12 * 2**20),
        name="plan",
    )(margin, ccd_first, from_chip, science)
    from_next, from_two, from_far, planned = lax.optimization_barrier((from_next, from_two, from_far, planned))
    plan, *tables = planned
    relay = jnp.concatenate([from_next[:NEAR_ROWS], from_two], axis=0)
    from_across = lax.ppermute(relay, "visit", on_chip)

    return pl.pallas_call(
        functools.partial(match_kernel, per_strip),
        out_shape=jax.ShapeDtypeStruct(patches.shape, f32),
        in_specs=[smem] + [vmem] * 10,
        out_specs=vmem,
        scratch_shapes=[
            pltpu.VMEM((MEMBERS * RECORD + EDGE, TILE), bf16),
            pltpu.VMEM((2, 2 * (TILE + 2 * EDGE), TILE), bf16),
            pltpu.VMEM((2, columns * REACH, TILE), bf16),
            pltpu.VMEM((HALF, columns * REACH), bf16),
            pltpu.VMEM((2, TILE, TILE), f32),
        ],
        compiler_params=pltpu.CompilerParams(vmem_limit_bytes=24 * 2**20),
        name="match",
    )(plan, aligned, to_chip, from_chip, from_next, from_two, from_across, from_far, *tables)


def solution(mesh):
    in_specs = (
        P(("grp", "visit"), None),
        P(("grp", "visit"), None, None),
        P("grp", None),
        P(None, ("grp", "visit")),
        P("grp"),
    )
    out_specs = P(("grp", "visit"), None, None)
    return jax.shard_map(step, mesh=mesh, in_specs=in_specs, out_specs=out_specs, check_vma=False)
```

profile of v0, /device:TPU:21, one launch (start us, length us, event | category | flops | bytes accessed | tf_op | source)
XLA Modules:
  0.0 28.3 jit_solution(1192202174099235472)
XLA Ops:
  0.0 0.0 copy-start
  0.0 0.0 copy-start.1
  0.0 0.8 %copy-done.1 = s32[64,3]{0,1:T(4,128)S(1)} copy-done((s32[64,3]{0,1:T(4,128)S(1)}, s32[64,3]{0,1:T(4,128)}, u32[]{:S(2)}) %copy-start.1) | copy-done | bytes 792
  0.8 0.0 copy-start.2
  0.8 0.7 %copy-done.2 = f32[27,4]{0,1:T(4,128)S(1)} copy-done((f32[27,4]{0,1:T(4,128)S(1)}, f32[27,4]{0,1:T(4,128)}, u32[]{:S(2)}) %copy-start.2) | copy-done | bytes 456
  1.5 0.0 copy-start.3
  1.5 3.3 %pack.1 = (bf16[6,256,256]{2,1,0:T(8,128)(2,1)S(1)}, bf16[912,256]{1,0:T(8,128)(2,1)S(1)}, bf16[688,256]{1,0:T(8,128)(2,1)S(1)}, bf16[80,256]{1,0:T(8,128)(2,1)S(1)}, bf16[32,256]{1,0:T(8,128)(2,1)S(1)}) custom-call(s32[3,64]{1,0:T(4,128)S(1)} %bitcast.2, f32[4,27]{1,0:T(4,128)S(1)} %bitcast.4, f32[8,256,256]{2,1,0:T(8,128)} %patches.1, f32[256,1024]{1,0:T(8,128)} %science.3), custom_call_target="tpu_custom_call" | custom-call | tf_op jit(solution)/shard_map/pack/pallas_call | solution.py:458
  4.8 0.7 %collective-permute-start.3 = (bf16[912,256]{1,0:T(8,128)(2,1)S(1)}, bf16[912,256]{1,0:T(8,128)(2,1)S(1)}, u32[]{:S(2)}, u32[]{:S(2)}) collective-permute-start(bf16[912,256]{1,0:T(8,128)(2,1)S(1)} %get-tuple-element.24.own_record), channel_id=1, source_target_pairs={{0,1},{1,0},{2,3},{3,2},{4,5},{5,4},{6,7},{7,6},{8,9},{9,8},{10,11... | collective-permute-start | bytes 1400840 | tf_op jit(solution)/shard_map/ppermute | solution.py:490
  5.4 2.6 %collective-permute-start = (bf16[688,256]{1,0:T(8,128)(2,1)S(1)}, bf16[688,256]{1,0:T(8,128)(2,1)S(1)}, u32[]{:S(2)}, u32[]{:S(2)}) collective-permute-start(bf16[688,256]{1,0:T(8,128)(2,1)S(1)} %get-tuple-element.21), channel_id=1, source_target_pairs={{1,2},{2,1},{3,4},{4,3},{5,6},{6,5},{7,8},{8,7},{9,10},{10,9},{11,... | collective-permute-start | bytes 1056776 | tf_op jit(solution)/shard_map/ppermute | solution.py:487
  8.0 3.5 %collective-permute-start.1 = (bf16[80,256]{1,0:T(8,128)(2,1)S(1)}, bf16[80,256]{1,0:T(8,128)(2,1)S(1)}, u32[]{:S(2)}, u32[]{:S(2)}) collective-permute-start(bf16[80,256]{1,0:T(8,128)(2,1)S(1)} %get-tuple-element.22), channel_id=1, source_target_pairs={{0,2},{3,1},{2,4},{5,3},{4,6},{7,5},{6,8},{9,7},{8,10},{11,9},{10,... | collective-permute-start | bytes 122888 | tf_op jit(solution)/shard_map/ppermute | solution.py:488
  11.5 2.8 %collective-permute-start.2 = (bf16[32,256]{1,0:T(8,128)(2,1)S(1)}, bf16[32,256]{1,0:T(8,128)(2,1)S(1)}, u32[]{:S(2)}, u32[]{:S(2)}) collective-permute-start(bf16[32,256]{1,0:T(8,128)(2,1)S(1)} %get-tuple-element.23), channel_id=1, source_target_pairs={{1,4},{4,1},{3,6},{6,3},{5,8},{8,5},{7,10},{10,7},{9,12},{12,9},{1... | collective-permute-start | bytes 49160 | tf_op jit(solution)/shard_map/ppermute | solution.py:489
  14.3 0.0 collective-permute-done.3.from_chip
  14.3 0.0 copy-done
  14.3 0.0 copy-done.3
  14.3 2.7 %plan.1 = (s32[128]{0:T(128)S(1)}, bf16[256,1152]{1,0:T(8,128)(2,1)S(1)}, f32[3,128,1440]{2,1,0:T(8,128)S(1)}, f32[8,256,256]{2,1,0:T(8,128)S(1)}) custom-call(s32[3,64]{1,0:T(4,128)S(1)} %bitcast.3, s32[16]{0:T(128)S(1)} %copy-done.3, bf16[912,256]{1,0:T(8,128)(2,1)S(1)} %collective-permute-done.3.from_chip, f32[256,1024]{1,0:T(8,128)S(1)} %copy-done), custom_call_target="tpu_custom_call" | custom-call | tf_op jit(solution)/shard_map/plan/pallas_call | solution.py:493
  17.1 0.0 collective-permute-done.2.from_far
  17.1 0.0 collective-permute-done.1.from_two
  17.1 1.6 %collective-permute-done.from_next = bf16[688,256]{1,0:T(8,128)(2,1)S(1)} collective-permute-done((bf16[688,256]{1,0:T(8,128)(2,1)S(1)}, bf16[688,256]{1,0:T(8,128)(2,1)S(1)}, u32[]{:S(2)}, u32[]{:S(2)}) %collective-permute-start) | collective-permute-done | bytes 352288 | tf_op jit(solution)/shard_map/ppermute | solution.py:487
  18.7 0.1 collective-permute-start.4
  18.8 1.3 %collective-permute-done.4.from_across = bf16[256,256]{1,0:T(8,128)(2,1)S(1)} collective-permute-done((bf16[256,256]{1,0:T(8,128)(2,1)S(1)}, bf16[256,256]{1,0:T(8,128)(2,1)S(1)}, u32[]{:S(2)}, u32[]{:S(2)}) %collective-permute-start.4) | collective-permute-done | bytes 131104 | tf_op jit(solution)/shard_map/ppermute | solution.py:510
  20.2 8.1 %match.1 = f32[8,256,256]{2,1,0:T(8,128)} custom-call(s32[128]{0:T(128)S(1)} %get-tuple-element.29.plan, bf16[6,256,256]{2,1,0:T(8,128)(2,1)S(1)} %get-tuple-element.30.aligned, bf16[912,256]{1,0:T(8,128)(2,1)S(1)} %get-tuple-element.24.own_record, bf16[912,256]{1,0:T(8,128)(2,1)S(1)} %collective-permute-done.3.from_chip, ...), custom_call_target="tpu_custom_call" | custom-call | tf_op jit(solution)/shard_map/match/pallas_call | solution.py:512
  (2 shorter events, 0.0 us)
Async XLA Ops:
  0.0 14.3 %copy-start = (f32[256,1024]{1,0:T(8,128)S(1)}, f32[256,1024]{1,0:T(8,128)}, u32[]{:S(2)}) copy-start(f32[256,1024]{1,0:T(8,128)} %science.3) | copy-start | bytes 3145732
  0.0 0.8 %copy-start.1 = (s32[64,3]{0,1:T(4,128)S(1)}, s32[64,3]{0,1:T(4,128)}, u32[]{:S(2)}) copy-start(s32[64,3]{0,1:T(4,128)} %param.7) | copy-start | bytes 2308
  0.8 0.7 %copy-start.2 = (f32[27,4]{0,1:T(4,128)S(1)}, f32[27,4]{0,1:T(4,128)}, u32[]{:S(2)}) copy-start(f32[27,4]{0,1:T(4,128)} %param.8) | copy-start | bytes 1300
  1.5 12.9 %copy-start.3 = (s32[16]{0:T(128)S(1)}, s32[16]{0:T(128)}, u32[]{:S(2)}) copy-start(s32[16]{0:T(128)} %ccd_first.1) | copy-start | bytes 196
  4.8 9.6 %collective-permute-start.3 = (bf16[912,256]{1,0:T(8,128)(2,1)S(1)}, bf16[912,256]{1,0:T(8,128)(2,1)S(1)}, u32[]{:S(2)}, u32[]{:S(2)}) collective-permute-start(bf16[912,256]{1,0:T(8,128)(2,1)S(1)} %get-tuple-element.24.own_record), channel_id=1, source_target_pairs={{0,1},{1,0},{2,3},{3,2},{4,5},{5,4},{6,7},{7,6},{8,9},{9,8},{10,11... | collective-permute-start | bytes 1400840 | tf_op jit(solution)/shard_map/ppermute | solution.py:490
  5.4 13.3 %collective-permute-start = (bf16[688,256]{1,0:T(8,128)(2,1)S(1)}, bf16[688,256]{1,0:T(8,128)(2,1)S(1)}, u32[]{:S(2)}, u32[]{:S(2)}) collective-permute-start(bf16[688,256]{1,0:T(8,128)(2,1)S(1)} %get-tuple-element.21), channel_id=1, source_target_pairs={{1,2},{2,1},{3,4},{4,3},{5,6},{6,5},{7,8},{8,7},{9,10},{10,9},{11,... | collective-permute-start | bytes 1056776 | tf_op jit(solution)/shard_map/ppermute | solution.py:487
  8.0 9.1 %collective-permute-start.1 = (bf16[80,256]{1,0:T(8,128)(2,1)S(1)}, bf16[80,256]{1,0:T(8,128)(2,1)S(1)}, u32[]{:S(2)}, u32[]{:S(2)}) collective-permute-start(bf16[80,256]{1,0:T(8,128)(2,1)S(1)} %get-tuple-element.22), channel_id=1, source_target_pairs={{0,2},{3,1},{2,4},{5,3},{4,6},{7,5},{6,8},{9,7},{8,10},{11,9},{10,... | collective-permute-start | bytes 122888 | tf_op jit(solution)/shard_map/ppermute | solution.py:488
  11.5 5.5 %collective-permute-start.2 = (bf16[32,256]{1,0:T(8,128)(2,1)S(1)}, bf16[32,256]{1,0:T(8,128)(2,1)S(1)}, u32[]{:S(2)}, u32[]{:S(2)}) collective-permute-start(bf16[32,256]{1,0:T(8,128)(2,1)S(1)} %get-tuple-element.23), channel_id=1, source_target_pairs={{1,4},{4,1},{3,6},{6,3},{5,8},{8,5},{7,10},{10,7},{9,12},{12,9},{1... | collective-permute-start | bytes 49160 | tf_op jit(solution)/shard_map/ppermute | solution.py:489
  18.7 1.4 %collective-permute-start.4 = (bf16[256,256]{1,0:T(8,128)(2,1)S(1)}, bf16[256,256]{1,0:T(8,128)(2,1)S(1)}, u32[]{:S(2)}, u32[]{:S(2)}) collective-permute-start(bf16[256,256]{1,0:T(8,128)(2,1)S(1)} %pad_maximum_fusion), channel_id=1, source_target_pairs={{0,1},{1,0},{2,3},{3,2},{4,5},{5,4},{6,7},{7,6},{8,9},{9,8},{10,11... | collective-permute-start | bytes 393224 | tf_op jit(solution)/shard_map/ppermute | solution.py:510
where the time goes:
time: 28.5 us; the launch traced here: 28.3 us
  Pallas kernels  14.1 us (49%)
  starting transfers between devices  9.6 us (34%)
  waiting for transfers between devices  2.99 us (10%)
  local copies, waits for them, and re-layouts  1.47 us (5%)
    pallas_call x1, Pallas kernels, step(): pl.pallas_call(functools.partial(match_kernel, per_strip), out_shape=jax....  8.12 us
    ppermute x1, starting transfers between devices, step(): from_two = lax.ppermute(to_two, 'visit', two)  3.5 us
    pallas_call x1, Pallas kernels, step(): pl.pallas_call(functools.partial(pack_kernel, sizes), out_shape=(jax.Shap...  3.29 us
    ppermute x1, starting transfers between devices, step(): from_far = lax.ppermute(to_far, 'visit', far)  2.78 us
    pallas_call x1, Pallas kernels, step(): pl.pallas_call(functools.partial(plan_kernel, sizes), out_shape=(jax.Shap...  2.71 us
    ppermute x1, starting transfers between devices, step(): from_next = lax.ppermute(to_next, 'visit', next_chip)  2.58 us
    ppermute x1, waiting for transfers between devices, step(): from_next = lax.ppermute(to_next, 'visit', next_chip)  1.65 us
    unnamed x8, local copies, waits for them, and re-layouts  1.46 us
  transfers between devices with their start and end apart: 5, of which 2 were waited for; matrix products, arithmetic and copies ran while one was open for 0% of the time, Pallas kernels for 10%

commit v1 on v0

--- a/solution.py
+++ b/solution.py
@@ -229,6 +229,8 @@
         plan[k] = slots[k]
         plan[SLOTS + k] = counts[k]
         plan[2 * SLOTS + k] = places[k]
+        later = sum((jnp.where(other == ids[k], 1, 0) for other in ids[k + 1 :]), jnp.int32(0))
+        plan[3 * SLOTS + 1 + k] = later
     plan[3 * SLOTS] = entry
 
     for i in range(2 * STRIPS - 1):
@@ -283,6 +285,7 @@
             plan[at + 12] = plan[SLOTS + k]
             plan[at + 13] = member + 3
             plan[at + 14] = position
+            plan[at + 15] = plan[3 * SLOTS + 1 + k]
             share = share_of(plan[SLOTS + k])
 
             @pl.when(member == 0)
@@ -311,8 +314,8 @@
 
 
 def match_kernel(per_strip, plan, aligned, own_record, from_chip, from_next, from_two, from_across, from_far,
-                 across, mixing, first, out,
-                 frames, window, spread, mixes, total):
+                 across, mixing, first, result,
+                 frames, window, spread, mixes, total, out, sems):
     def put(member, start, rows, value):
         frames[member * RECORD + start : member * RECORD + start + rows, :] = value
 
@@ -378,6 +381,10 @@
         out[local] = out[local] - back * share
 
     count = plan[3 * SLOTS]
+    owned = out.shape[0]
+
+    def leave(local):
+        return pltpu.make_async_copy(out.at[local], result.at[local], sems.at[local])
 
     for k in range(SLOTS):
         @pl.when((plan[k] >= 0) & (plan[base(plan[2 * SLOTS + k]) + 13] == 2))
@@ -387,6 +394,15 @@
             start = NEAR_ROWS + (k % CAP) * TILE
             arrived = from_next[start : start + TILE, :].astype(jnp.float32)
             out[local] = out[local] + arrived * share_of(plan[at + 12])
+
+    for local in range(owned):
+        named = sum(
+            jnp.where((plan[k] >= 0) & (plan[base(plan[2 * SLOTS + k]) + 11] == local), 1, 0) for k in range(SLOTS)
+        )
+
+        @pl.when(named == 0)
+        def _(local=local):
+            leave(local).start()
 
     @pl.when(count > 0)
     def _():
@@ -434,6 +450,12 @@
             total[half, r * HALF : (r + 1) * HALF, :] = jnp.dot(
                 mixes[...], spread[r], preferred_element_type=jnp.float32
             )
+        before = base(jnp.maximum(k - 1, 0))
+
+        @pl.when((k > 0) & (plan[before + 15] == 0))
+        def _():
+            leave(plan[before + 11]).start()
+
         return carry
 
     lax.fori_loop(0, count, step, 0)
@@ -441,6 +463,10 @@
     @pl.when(count > 0)
     def _():
         finish(count - 1, lax.rem(count - 1, 2), share_of(plan[base(count - 1) + 12]))
+        leave(plan[base(count - 1) + 11]).start()
+
+    for local in range(owned):
+        leave(local).wait()
 
 
 def step(science, patches, margin, kernel_coef, ccd_first):
@@ -513,13 +539,15 @@
         functools.partial(match_kernel, per_strip),
         out_shape=jax.ShapeDtypeStruct(patches.shape, f32),
         in_specs=[smem] + [vmem] * 10,
-        out_specs=vmem,
+        out_specs=stays,
         scratch_shapes=[
             pltpu.VMEM((MEMBERS * RECORD + EDGE, TILE), bf16),
             pltpu.VMEM((2, 2 * (TILE + 2 * EDGE), TILE), bf16),
             pltpu.VMEM((2, columns * REACH, TILE), bf16),
             pltpu.VMEM((HALF, columns * REACH), bf16),
             pltpu.VMEM((2, TILE, TILE), f32),
+            pltpu.VMEM(patches.shape, f32),
+            pltpu.SemaphoreType.DMA((patches.shape[0],)),
         ],
         compiler_params=pltpu.CompilerParams(vmem_limit_bytes=24 * 2**20),
         name="match",

time: 28.5 us -> 28.1 us (0.986)
  Pallas kernels: 14.1 us -> 13.7 us
    pallas_call x1, Pallas kernels: 8.12 us -> 7.69 us  [step(): pl.pallas_call(functools.partial(match_kernel, per_strip), out_shape=jax....]
where the time goes in v1:
time: 28.1 us; the launch traced here: 27.8 us
  Pallas kernels  13.7 us (49%)
  starting transfers between devices  9.6 us (34%)
  waiting for transfers between devices  2.96 us (11%)
  local copies, waits for them, and re-layouts  1.47 us (5%)
    pallas_call x1, Pallas kernels, step(): pl.pallas_call(functools.partial(match_kernel, per_strip), out_shape=jax....  7.69 us
    ppermute x1, starting transfers between devices, step(): from_two = lax.ppermute(to_two, 'visit', two)  3.5 us
    pallas_call x1, Pallas kernels, step(): pl.pallas_call(functools.partial(pack_kernel, sizes), out_shape=(jax.Shap...  3.29 us
    ppermute x1, starting transfers between devices, step(): from_far = lax.ppermute(to_far, 'visit', far)  2.78 us
    pallas_call x1, Pallas kernels, step(): pl.pallas_call(functools.partial(plan_kernel, sizes), out_shape=(jax.Shap...  2.74 us
    ppermute x1, starting transfers between devices, step(): from_next = lax.ppermute(to_next, 'visit', next_chip)  2.58 us
    ppermute x1, waiting for transfers between devices, step(): from_next = lax.ppermute(to_next, 'visit', next_chip)  1.62 us
    unnamed x8, local copies, waits for them, and re-layouts  1.46 us
  transfers between devices with their start and end apart: 5, of which 2 were waited for; matrix products, arithmetic and copies ran while one was open for 0% of the time, Pallas kernels for 10%

profile of v1, /device:TPU:21, one launch (start us, length us, event | category | flops | bytes accessed | tf_op | source)
XLA Modules:
  0.0 27.8 jit_solution(1923544959263286861)
XLA Ops:
  0.0 0.0 copy-start
  0.0 0.0 copy-start.1
  0.0 0.8 %copy-done.1 = s32[64,3]{0,1:T(4,128)S(1)} copy-done((s32[64,3]{0,1:T(4,128)S(1)}, s32[64,3]{0,1:T(4,128)}, u32[]{:S(2)}) %copy-start.1) | copy-done | bytes 792
  0.8 0.0 copy-start.2
  0.8 0.7 %copy-done.2 = f32[27,4]{0,1:T(4,128)S(1)} copy-done((f32[27,4]{0,1:T(4,128)S(1)}, f32[27,4]{0,1:T(4,128)}, u32[]{:S(2)}) %copy-start.2) | copy-done | bytes 456
  1.5 0.0 copy-start.3
  1.5 3.3 %pack.1 = (bf16[6,256,256]{2,1,0:T(8,128)(2,1)S(1)}, bf16[912,256]{1,0:T(8,128)(2,1)S(1)}, bf16[688,256]{1,0:T(8,128)(2,1)S(1)}, bf16[80,256]{1,0:T(8,128)(2,1)S(1)}, bf16[32,256]{1,0:T(8,128)(2,1)S(1)}) custom-call(s32[3,64]{1,0:T(4,128)S(1)} %bitcast.2, f32[4,27]{1,0:T(4,128)S(1)} %bitcast.4, f32[8,256,256]{2,1,0:T(8,128)} %patches.1, f32[256,1024]{1,0:T(8,128)} %science.3), custom_call_target="tpu_custom_call" | custom-call | tf_op jit(solution)/shard_map/pack/pallas_call | solution.py:484
  4.8 0.7 %collective-permute-start.3 = (bf16[912,256]{1,0:T(8,128)(2,1)S(1)}, bf16[912,256]{1,0:T(8,128)(2,1)S(1)}, u32[]{:S(2)}, u32[]{:S(2)}) collective-permute-start(bf16[912,256]{1,0:T(8,128)(2,1)S(1)} %get-tuple-element.24.own_record), channel_id=1, source_target_pairs={{0,1},{1,0},{2,3},{3,2},{4,5},{5,4},{6,7},{7,6},{8,9},{9,8},{10,11... | collective-permute-start | bytes 1400840 | tf_op jit(solution)/shard_map/ppermute | solution.py:516
  5.4 2.6 %collective-permute-start = (bf16[688,256]{1,0:T(8,128)(2,1)S(1)}, bf16[688,256]{1,0:T(8,128)(2,1)S(1)}, u32[]{:S(2)}, u32[]{:S(2)}) collective-permute-start(bf16[688,256]{1,0:T(8,128)(2,1)S(1)} %get-tuple-element.21), channel_id=1, source_target_pairs={{1,2},{2,1},{3,4},{4,3},{5,6},{6,5},{7,8},{8,7},{9,10},{10,9},{11,... | collective-permute-start | bytes 1056776 | tf_op jit(solution)/shard_map/ppermute | solution.py:513
  8.0 3.5 %collective-permute-start.1 = (bf16[80,256]{1,0:T(8,128)(2,1)S(1)}, bf16[80,256]{1,0:T(8,128)(2,1)S(1)}, u32[]{:S(2)}, u32[]{:S(2)}) collective-permute-start(bf16[80,256]{1,0:T(8,128)(2,1)S(1)} %get-tuple-element.22), channel_id=1, source_target_pairs={{0,2},{3,1},{2,4},{5,3},{4,6},{7,5},{6,8},{9,7},{8,10},{11,9},{10,... | collective-permute-start | bytes 122888 | tf_op jit(solution)/shard_map/ppermute | solution.py:514
  11.5 2.8 %collective-permute-start.2 = (bf16[32,256]{1,0:T(8,128)(2,1)S(1)}, bf16[32,256]{1,0:T(8,128)(2,1)S(1)}, u32[]{:S(2)}, u32[]{:S(2)}) collective-permute-start(bf16[32,256]{1,0:T(8,128)(2,1)S(1)} %get-tuple-element.23), channel_id=1, source_target_pairs={{1,4},{4,1},{3,6},{6,3},{5,8},{8,5},{7,10},{10,7},{9,12},{12,9},{1... | collective-permute-start | bytes 49160 | tf_op jit(solution)/shard_map/ppermute | solution.py:515
  14.3 0.0 collective-permute-done.3.from_chip
  14.3 0.0 copy-done
  14.3 0.0 copy-done.3
  14.3 2.7 %plan.1 = (s32[128]{0:T(128)S(1)}, bf16[256,1152]{1,0:T(8,128)(2,1)S(1)}, f32[3,128,1440]{2,1,0:T(8,128)S(1)}, f32[8,256,256]{2,1,0:T(8,128)S(1)}) custom-call(s32[3,64]{1,0:T(4,128)S(1)} %bitcast.3, s32[16]{0:T(128)S(1)} %copy-done.3, bf16[912,256]{1,0:T(8,128)(2,1)S(1)} %collective-permute-done.3.from_chip, f32[256,1024]{1,0:T(8,128)S(1)} %copy-done), custom_call_target="tpu_custom_call" | custom-call | tf_op jit(solution)/shard_map/plan/pallas_call | solution.py:519
  17.1 0.0 collective-permute-done.2.from_far
  17.1 0.0 collective-permute-done.1.from_two
  17.1 1.6 %collective-permute-done.from_next = bf16[688,256]{1,0:T(8,128)(2,1)S(1)} collective-permute-done((bf16[688,256]{1,0:T(8,128)(2,1)S(1)}, bf16[688,256]{1,0:T(8,128)(2,1)S(1)}, u32[]{:S(2)}, u32[]{:S(2)}) %collective-permute-start) | collective-permute-done | bytes 352288 | tf_op jit(solution)/shard_map/ppermute | solution.py:513
  18.7 0.1 collective-permute-start.4
  18.8 1.3 %collective-permute-done.4.from_across = bf16[256,256]{1,0:T(8,128)(2,1)S(1)} collective-permute-done((bf16[256,256]{1,0:T(8,128)(2,1)S(1)}, bf16[256,256]{1,0:T(8,128)(2,1)S(1)}, u32[]{:S(2)}, u32[]{:S(2)}) %collective-permute-start.4) | collective-permute-done | bytes 131104 | tf_op jit(solution)/shard_map/ppermute | solution.py:536
  20.2 7.7 %match.1 = f32[8,256,256]{2,1,0:T(8,128)} custom-call(s32[128]{0:T(128)S(1)} %get-tuple-element.29.plan, bf16[6,256,256]{2,1,0:T(8,128)(2,1)S(1)} %get-tuple-element.30.aligned, bf16[912,256]{1,0:T(8,128)(2,1)S(1)} %get-tuple-element.24.own_record, bf16[912,256]{1,0:T(8,128)(2,1)S(1)} %collective-permute-done.3.from_chip, ...), custom_call_target="tpu_custom_call" | custom-call | tf_op jit(solution)/shard_map/match/pallas_call | solution.py:538
  (2 shorter events, 0.0 us)
Async XLA Ops:
  0.0 14.3 %copy-start = (f32[256,1024]{1,0:T(8,128)S(1)}, f32[256,1024]{1,0:T(8,128)}, u32[]{:S(2)}) copy-start(f32[256,1024]{1,0:T(8,128)} %science.3) | copy-start | bytes 3145732
  0.0 0.8 %copy-start.1 = (s32[64,3]{0,1:T(4,128)S(1)}, s32[64,3]{0,1:T(4,128)}, u32[]{:S(2)}) copy-start(s32[64,3]{0,1:T(4,128)} %param.7) | copy-start | bytes 2308
  0.8 0.7 %copy-start.2 = (f32[27,4]{0,1:T(4,128)S(1)}, f32[27,4]{0,1:T(4,128)}, u32[]{:S(2)}) copy-start(f32[27,4]{0,1:T(4,128)} %param.8) | copy-start | bytes 1300
  1.5 12.9 %copy-start.3 = (s32[16]{0:T(128)S(1)}, s32[16]{0:T(128)}, u32[]{:S(2)}) copy-start(s32[16]{0:T(128)} %ccd_first.1) | copy-start | bytes 196
  4.8 9.6 %collective-permute-start.3 = (bf16[912,256]{1,0:T(8,128)(2,1)S(1)}, bf16[912,256]{1,0:T(8,128)(2,1)S(1)}, u32[]{:S(2)}, u32[]{:S(2)}) collective-permute-start(bf16[912,256]{1,0:T(8,128)(2,1)S(1)} %get-tuple-element.24.own_record), channel_id=1, source_target_pairs={{0,1},{1,0},{2,3},{3,2},{4,5},{5,4},{6,7},{7,6},{8,9},{9,8},{10,11... | collective-permute-start | bytes 1400840 | tf_op jit(solution)/shard_map/ppermute | solution.py:516
  5.4 13.3 %collective-permute-start = (bf16[688,256]{1,0:T(8,128)(2,1)S(1)}, bf16[688,256]{1,0:T(8,128)(2,1)S(1)}, u32[]{:S(2)}, u32[]{:S(2)}) collective-permute-start(bf16[688,256]{1,0:T(8,128)(2,1)S(1)} %get-tuple-element.21), channel_id=1, source_target_pairs={{1,2},{2,1},{3,4},{4,3},{5,6},{6,5},{7,8},{8,7},{9,10},{10,9},{11,... | collective-permute-start | bytes 1056776 | tf_op jit(solution)/shard_map/ppermute | solution.py:513
  8.0 9.1 %collective-permute-start.1 = (bf16[80,256]{1,0:T(8,128)(2,1)S(1)}, bf16[80,256]{1,0:T(8,128)(2,1)S(1)}, u32[]{:S(2)}, u32[]{:S(2)}) collective-permute-start(bf16[80,256]{1,0:T(8,128)(2,1)S(1)} %get-tuple-element.22), channel_id=1, source_target_pairs={{0,2},{3,1},{2,4},{5,3},{4,6},{7,5},{6,8},{9,7},{8,10},{11,9},{10,... | collective-permute-start | bytes 122888 | tf_op jit(solution)/shard_map/ppermute | solution.py:514
  11.5 5.6 %collective-permute-start.2 = (bf16[32,256]{1,0:T(8,128)(2,1)S(1)}, bf16[32,256]{1,0:T(8,128)(2,1)S(1)}, u32[]{:S(2)}, u32[]{:S(2)}) collective-permute-start(bf16[32,256]{1,0:T(8,128)(2,1)S(1)} %get-tuple-element.23), channel_id=1, source_target_pairs={{1,4},{4,1},{3,6},{6,3},{5,8},{8,5},{7,10},{10,7},{9,12},{12,9},{1... | collective-permute-start | bytes 49160 | tf_op jit(solution)/shard_map/ppermute | solution.py:515
  18.7 1.4 %collective-permute-start.4 = (bf16[256,256]{1,0:T(8,128)(2,1)S(1)}, bf16[256,256]{1,0:T(8,128)(2,1)S(1)}, u32[]{:S(2)}, u32[]{:S(2)}) collective-permute-start(bf16[256,256]{1,0:T(8,128)(2,1)S(1)} %pad_maximum_fusion), channel_id=1, source_target_pairs={{0,1},{1,0},{2,3},{3,2},{4,5},{5,4},{6,7},{7,6},{8,9},{9,8},{10,11... | collective-permute-start | bytes 393224 | tf_op jit(solution)/shard_map/ppermute | solution.py:536

commit v2 on v1

--- a/solution.py
+++ b/solution.py
@@ -214,7 +214,7 @@
             shape = shape * (u / sigma)
 
 
-def plan_kernel(sizes, margin, ccd_first, from_chip, science, plan, across, mixing, first, rows):
+def plan_kernel(sizes, margin, ccd_first, from_chip, science, plan, first, rows):
     strips, per_strip, owned = sizes
     owner = lax.axis_index("visit")
     sign = sign_of(owner)
@@ -303,7 +303,6 @@
 
     first[...] = jnp.zeros(first.shape, jnp.float32)
     lax.fori_loop(0, SLOTS, fill, 0)
-    fill_tables(across, mixing)
 
 
 def share_of(count):
@@ -481,6 +480,19 @@
     stays = pl.BlockSpec(memory_space=pltpu.HBM)
     bf16 = jnp.bfloat16
     f32 = jnp.float32
+    columns = SIGMAS * ORDERS
+    tables = pl.pallas_call(
+        fill_tables,
+        out_shape=(
+            jax.ShapeDtypeStruct((TILE, columns * HALF), bf16),
+            jax.ShapeDtypeStruct((ORDERS, HALF, columns * REACH), f32),
+        ),
+        in_specs=[],
+        out_specs=(vmem, vmem),
+        compiler_params=pltpu.CompilerParams(vmem_limit_bytes=8 * 2**20),
+        cost_estimate=pl.CostEstimate(flops=2 * 10**9, bytes_accessed=3 * 2**20, transcendentals=10**6),
+        name="tables",
+    )()
     aligned, to_chip, to_next, to_two, to_far = pl.pallas_call(
         functools.partial(pack_kernel, sizes),
         out_shape=(
@@ -515,23 +527,20 @@
     from_far = lax.ppermute(to_far, "visit", far)
     from_chip = lax.ppermute(to_chip, "visit", on_chip)
 
-    columns = SIGMAS * ORDERS
     planned = pl.pallas_call(
         functools.partial(plan_kernel, sizes),
         out_shape=(
             jax.ShapeDtypeStruct((ENTRY * (HEAD + SLOTS),), jnp.int32),
-            jax.ShapeDtypeStruct((TILE, columns * HALF), bf16),
-            jax.ShapeDtypeStruct((ORDERS, HALF, columns * REACH), f32),
             jax.ShapeDtypeStruct(patches.shape, f32),
         ),
         in_specs=[smem, smem] + [vmem] * 2,
-        out_specs=(smem, vmem, vmem, vmem),
+        out_specs=(smem, vmem),
         scratch_shapes=[pltpu.SMEM(((2 * STRIPS - 1) * per_strip * KINDS,), jnp.int32)],
         compiler_params=pltpu.CompilerParams(vmem_limit_bytes=12 * 2**20),
         name="plan",
     )(margin, ccd_first, from_chip, science)
     from_next, from_two, from_far, planned = lax.optimization_barrier((from_next, from_two, from_far, planned))
-    plan, *tables = planned
+    plan, first = planned
     relay = jnp.concatenate([from_next[:NEAR_ROWS], from_two], axis=0)
     from_across = lax.ppermute(relay, "visit", on_chip)
 
@@ -551,7 +560,7 @@
         ],
         compiler_params=pltpu.CompilerParams(vmem_limit_bytes=24 * 2**20),
         name="match",
-    )(plan, aligned, to_chip, from_chip, from_next, from_two, from_across, from_far, *tables)
+    )(plan, aligned, to_chip, from_chip, from_next, from_two, from_across, from_far, *tables, first)
 
 
 def solution(mesh):

time: 28.1 us -> 28.1 us (level)
  Pallas kernels: 13.7 us -> 14.3 us
  waiting for transfers between devices: 2.96 us -> 2.38 us
    ppermute x1, waiting for transfers between devices: 1.33 us -> 0.62 us  [step(): from_across = lax.ppermute(relay, 'visit', on_chip)]
    pallas_call x0 -> x1, Pallas kernels: none -> 0.71 us  [step(): pl.pallas_call(fill_tables, out_shape=(jax.ShapeDtypeStruct((TILE, column...]
  transfers between devices with their start and end apart: 5 -> 5, of which waited for: 2 -> 2; matrix products, arithmetic and copies ran while one was open for 0% -> 0% of each run, Pallas kernels for 10% -> 12%
where the time goes in v2:
time: 28.1 us; the launch traced here: 27.8 us
  Pallas kernels  14.3 us (51%)
  starting transfers between devices  9.6 us (34%)
  waiting for transfers between devices  2.38 us (8%)
  local copies, waits for them, and re-layouts  1.47 us (5%)
    pallas_call x1, Pallas kernels, step(): pl.pallas_call(functools.partial(match_kernel, per_strip), out_shape=jax....  7.69 us
    ppermute x1, starting transfers between devices, step(): from_two = lax.ppermute(to_two, 'visit', two)  3.5 us
    pallas_call x1, Pallas kernels, step(): pl.pallas_call(functools.partial(pack_kernel, sizes), out_shape=(jax.Shap...  3.29 us
    ppermute x1, starting transfers between devices, step(): from_far = lax.ppermute(to_far, 'visit', far)  2.78 us
    pallas_call x1, Pallas kernels, step(): pl.pallas_call(functools.partial(plan_kernel, sizes), out_shape=(jax.Shap...  2.61 us
    ppermute x1, starting transfers between devices, step(): from_next = lax.ppermute(to_next, 'visit', next_chip)  2.58 us
    ppermute x1, waiting for transfers between devices, step(): from_next = lax.ppermute(to_next, 'visit', next_chip)  1.74 us
    unnamed x8, local copies, waits for them, and re-layouts  1.46 us
  transfers between devices with their start and end apart: 5, of which 2 were waited for; matrix products, arithmetic and copies ran while one was open for 0% of the time, Pallas kernels for 12%

profile of v2, /device:TPU:21, one launch (start us, length us, event | category | flops | bytes accessed | tf_op | source)
XLA Modules:
  0.0 27.8 jit_solution(7665265572867878345)
XLA Ops:
  0.0 0.0 copy-start
  0.0 0.0 copy-start.1
  0.0 0.8 %copy-done.1 = s32[64,3]{0,1:T(4,128)S(1)} copy-done((s32[64,3]{0,1:T(4,128)S(1)}, s32[64,3]{0,1:T(4,128)}, u32[]{:S(2)}) %copy-start.1) | copy-done | bytes 792
  0.8 0.0 copy-start.2
  0.8 0.7 %copy-done.2 = f32[27,4]{0,1:T(4,128)S(1)} copy-done((f32[27,4]{0,1:T(4,128)S(1)}, f32[27,4]{0,1:T(4,128)}, u32[]{:S(2)}) %copy-start.2) | copy-done | bytes 456
  1.5 0.0 copy-start.3
  1.5 3.3 %pack.1 = (bf16[6,256,256]{2,1,0:T(8,128)(2,1)S(1)}, bf16[912,256]{1,0:T(8,128)(2,1)S(1)}, bf16[688,256]{1,0:T(8,128)(2,1)S(1)}, bf16[80,256]{1,0:T(8,128)(2,1)S(1)}, bf16[32,256]{1,0:T(8,128)(2,1)S(1)}) custom-call(s32[3,64]{1,0:T(4,128)S(1)} %bitcast.2, f32[4,27]{1,0:T(4,128)S(1)} %bitcast.4, f32[8,256,256]{2,1,0:T(8,128)} %patches.1, f32[256,1024]{1,0:T(8,128)} %science.3), custom_call_target="tpu_custom_call" | custom-call | tf_op jit(solution)/shard_map/pack/pallas_call | solution.py:496
  4.8 0.7 %collective-permute-start.3 = (bf16[912,256]{1,0:T(8,128)(2,1)S(1)}, bf16[912,256]{1,0:T(8,128)(2,1)S(1)}, u32[]{:S(2)}, u32[]{:S(2)}) collective-permute-start(bf16[912,256]{1,0:T(8,128)(2,1)S(1)} %get-tuple-element.22.own_record), channel_id=1, source_target_pairs={{0,1},{1,0},{2,3},{3,2},{4,5},{5,4},{6,7},{7,6},{8,9},{9,8},{10,11... | collective-permute-start | bytes 1400840 | tf_op jit(solution)/shard_map/ppermute | solution.py:528
  5.4 2.6 %collective-permute-start = (bf16[688,256]{1,0:T(8,128)(2,1)S(1)}, bf16[688,256]{1,0:T(8,128)(2,1)S(1)}, u32[]{:S(2)}, u32[]{:S(2)}) collective-permute-start(bf16[688,256]{1,0:T(8,128)(2,1)S(1)} %get-tuple-element.19), channel_id=1, source_target_pairs={{1,2},{2,1},{3,4},{4,3},{5,6},{6,5},{7,8},{8,7},{9,10},{10,9},{11,... | collective-permute-start | bytes 1056776 | tf_op jit(solution)/shard_map/ppermute | solution.py:525
  8.0 3.5 %collective-permute-start.1 = (bf16[80,256]{1,0:T(8,128)(2,1)S(1)}, bf16[80,256]{1,0:T(8,128)(2,1)S(1)}, u32[]{:S(2)}, u32[]{:S(2)}) collective-permute-start(bf16[80,256]{1,0:T(8,128)(2,1)S(1)} %get-tuple-element.20), channel_id=1, source_target_pairs={{0,2},{3,1},{2,4},{5,3},{4,6},{7,5},{6,8},{9,7},{8,10},{11,9},{10,... | collective-permute-start | bytes 122888 | tf_op jit(solution)/shard_map/ppermute | solution.py:526
  11.5 2.8 %collective-permute-start.2 = (bf16[32,256]{1,0:T(8,128)(2,1)S(1)}, bf16[32,256]{1,0:T(8,128)(2,1)S(1)}, u32[]{:S(2)}, u32[]{:S(2)}) collective-permute-start(bf16[32,256]{1,0:T(8,128)(2,1)S(1)} %get-tuple-element.21), channel_id=1, source_target_pairs={{1,4},{4,1},{3,6},{6,3},{5,8},{8,5},{7,10},{10,7},{9,12},{12,9},{1... | collective-permute-start | bytes 49160 | tf_op jit(solution)/shard_map/ppermute | solution.py:527
  14.3 0.0 collective-permute-done.3.from_chip
  14.3 0.0 copy-done
  14.3 0.0 copy-done.3
  14.3 2.6 %plan.1 = (s32[128]{0:T(128)S(1)}, f32[8,256,256]{2,1,0:T(8,128)S(1)}) custom-call(s32[3,64]{1,0:T(4,128)S(1)} %bitcast.3, s32[16]{0:T(128)S(1)} %copy-done.3, bf16[912,256]{1,0:T(8,128)(2,1)S(1)} %collective-permute-done.3.from_chip, f32[256,1024]{1,0:T(8,128)S(1)} %copy-done), custom_call_target="tpu_custom_call" | custom-call | tf_op jit(solution)/shard_map/plan/pallas_call | solution.py:530
  17.0 0.0 collective-permute-done.2.from_far
  17.0 0.0 collective-permute-done.1.from_two
  17.0 1.7 %collective-permute-done.from_next = bf16[688,256]{1,0:T(8,128)(2,1)S(1)} collective-permute-done((bf16[688,256]{1,0:T(8,128)(2,1)S(1)}, bf16[688,256]{1,0:T(8,128)(2,1)S(1)}, u32[]{:S(2)}, u32[]{:S(2)}) %collective-permute-start) | collective-permute-done | bytes 352288 | tf_op jit(solution)/shard_map/ppermute | solution.py:525
  18.7 0.1 collective-permute-start.4
  18.8 0.7 %tables.1 = (bf16[256,1152]{1,0:T(8,128)(2,1)S(1)}, f32[3,128,1440]{2,1,0:T(8,128)S(1)}) custom-call(), custom_call_target="tpu_custom_call" | custom-call | flops 2000000000 | bytes 3145728 | tf_op jit(solution)/shard_map/tables/pallas_call | solution.py:484
  19.5 0.6 %collective-permute-done.4.from_across = bf16[256,256]{1,0:T(8,128)(2,1)S(1)} collective-permute-done((bf16[256,256]{1,0:T(8,128)(2,1)S(1)}, bf16[256,256]{1,0:T(8,128)(2,1)S(1)}, u32[]{:S(2)}, u32[]{:S(2)}) %collective-permute-start.4) | collective-permute-done | bytes 131104 | tf_op jit(solution)/shard_map/ppermute | solution.py:545
  20.2 7.7 %match.1 = f32[8,256,256]{2,1,0:T(8,128)} custom-call(s32[128]{0:T(128)S(1)} %get-tuple-element.25.plan, bf16[6,256,256]{2,1,0:T(8,128)(2,1)S(1)} %get-tuple-element.26.aligned, bf16[912,256]{1,0:T(8,128)(2,1)S(1)} %get-tuple-element.22.own_record, bf16[912,256]{1,0:T(8,128)(2,1)S(1)} %collective-permute-done.3.from_chip, ...), custom_call_target="tpu_custom_call" | custom-call | tf_op jit(solution)/shard_map/match/pallas_call | solution.py:547
  (2 shorter events, 0.0 us)
Async XLA Ops:
  0.0 14.3 %copy-start = (f32[256,1024]{1,0:T(8,128)S(1)}, f32[256,1024]{1,0:T(8,128)}, u32[]{:S(2)}) copy-start(f32[256,1024]{1,0:T(8,128)} %science.3) | copy-start | bytes 3145732
  0.0 0.8 %copy-start.1 = (s32[64,3]{0,1:T(4,128)S(1)}, s32[64,3]{0,1:T(4,128)}, u32[]{:S(2)}) copy-start(s32[64,3]{0,1:T(4,128)} %param.7) | copy-start | bytes 2308
  0.8 0.7 %copy-start.2 = (f32[27,4]{0,1:T(4,128)S(1)}, f32[27,4]{0,1:T(4,128)}, u32[]{:S(2)}) copy-start(f32[27,4]{0,1:T(4,128)} %param.8) | copy-start | bytes 1300
  1.5 12.9 %copy-start.3 = (s32[16]{0:T(128)S(1)}, s32[16]{0:T(128)}, u32[]{:S(2)}) copy-start(s32[16]{0:T(128)} %ccd_first.1) | copy-start | bytes 196
  4.8 9.6 %collective-permute-start.3 = (bf16[912,256]{1,0:T(8,128)(2,1)S(1)}, bf16[912,256]{1,0:T(8,128)(2,1)S(1)}, u32[]{:S(2)}, u32[]{:S(2)}) collective-permute-start(bf16[912,256]{1,0:T(8,128)(2,1)S(1)} %get-tuple-element.22.own_record), channel_id=1, source_target_pairs={{0,1},{1,0},{2,3},{3,2},{4,5},{5,4},{6,7},{7,6},{8,9},{9,8},{10,11... | collective-permute-start | bytes 1400840 | tf_op jit(solution)/shard_map/ppermute | solution.py:528
  5.4 13.3 %collective-permute-start = (bf16[688,256]{1,0:T(8,128)(2,1)S(1)}, bf16[688,256]{1,0:T(8,128)(2,1)S(1)}, u32[]{:S(2)}, u32[]{:S(2)}) collective-permute-start(bf16[688,256]{1,0:T(8,128)(2,1)S(1)} %get-tuple-element.19), channel_id=1, source_target_pairs={{1,2},{2,1},{3,4},{4,3},{5,6},{6,5},{7,8},{8,7},{9,10},{10,9},{11,... | collective-permute-start | bytes 1056776 | tf_op jit(solution)/shard_map/ppermute | solution.py:525
  8.0 9.0 %collective-permute-start.1 = (bf16[80,256]{1,0:T(8,128)(2,1)S(1)}, bf16[80,256]{1,0:T(8,128)(2,1)S(1)}, u32[]{:S(2)}, u32[]{:S(2)}) collective-permute-start(bf16[80,256]{1,0:T(8,128)(2,1)S(1)} %get-tuple-element.20), channel_id=1, source_target_pairs={{0,2},{3,1},{2,4},{5,3},{4,6},{7,5},{6,8},{9,7},{8,10},{11,9},{10,... | collective-permute-start | bytes 122888 | tf_op jit(solution)/shard_map/ppermute | solution.py:526
  11.5 5.4 %collective-permute-start.2 = (bf16[32,256]{1,0:T(8,128)(2,1)S(1)}, bf16[32,256]{1,0:T(8,128)(2,1)S(1)}, u32[]{:S(2)}, u32[]{:S(2)}) collective-permute-start(bf16[32,256]{1,0:T(8,128)(2,1)S(1)} %get-tuple-element.21), channel_id=1, source_target_pairs={{1,4},{4,1},{3,6},{6,3},{5,8},{8,5},{7,10},{10,7},{9,12},{12,9},{1... | collective-permute-start | bytes 49160 | tf_op jit(solution)/shard_map/ppermute | solution.py:527
  18.7 1.4 %collective-permute-start.4 = (bf16[256,256]{1,0:T(8,128)(2,1)S(1)}, bf16[256,256]{1,0:T(8,128)(2,1)S(1)}, u32[]{:S(2)}, u32[]{:S(2)}) collective-permute-start(bf16[256,256]{1,0:T(8,128)(2,1)S(1)} %pad_maximum_fusion), channel_id=1, source_target_pairs={{0,1},{1,0},{2,3},{3,2},{4,5},{5,4},{6,7},{7,6},{8,9},{9,8},{10,11... | collective-permute-start | bytes 393224 | tf_op jit(solution)/shard_map/ppermute | solution.py:545
